TPU v7x, 128 devices: a whole 4x4x4 slice. The times are simulated.
128 devices in a mesh: hst: 4 (over z), dev: 32 (over y, x, core).
Axes of the slice: x: 4, y: 4, z: 4, core: 2. Of those that a mesh axis runs over, the one named last changes fastest.
Arguments:
- features: bfloat16 [262144, 768], P(('hst', 'dev')), may hold values from -6 to 6
- cache_blocks: bfloat16 [4, 8192, 768], P('hst', 'dev'), may hold values from -6 to 6
- plan: int32 [4, 64], P('hst', 'dev'), may hold values from 0 to 63, as said below
- miss_ids: int32 [128, 4, 32, 16], P(('hst', 'dev')), may hold values from 0 to 2303, as said below
- miss_counts: int32 [128, 4, 32], P(('hst', 'dev')), may hold values from 4 to 16, as said below
- self_ids: int32 [106496], P(('hst', 'dev')), may hold values from 0 to 2047, as said below
- nbr_ids: int32 [106496, 15], P(('hst', 'dev')), may hold values from 0 to 2047, as said below
- hop_counts: int32 [106496], P(('hst', 'dev')), may hold values from 1 to 15, as said below
- seed_counts: int32 [4096], P(('hst', 'dev')), may hold values from 1 to 25, as said below
- w_self1: bfloat16 [768, 1024], replicated, may hold values from -0.21875 to 0.21875
- w_nbr1: bfloat16 [768, 1024], replicated, may hold values from -0.21875 to 0.21875
- w_self2: bfloat16 [1024, 1024], replicated, may hold values from -0.1875 to 0.1875
- w_nbr2: bfloat16 [1024, 1024], replicated, may hold values from -0.1875 to 0.1875
- cotangent: bfloat16 [4096, 1024], P(('hst', 'dev')), may hold values from -1.25 to 1.25
Outputs:
- embedding: bfloat16 [4096, 1024], P(('hst', 'dev'))
- new_cache: bfloat16 [4, 8192, 768], P('hst', 'dev')
- grad_self1: float32 [768, 1024], P(None, ('hst', 'dev'))
- grad_nbr1: float32 [768, 1024], P(None, ('hst', 'dev'))
- grad_self2: float32 [1024, 1024], P(None, ('hst', 'dev'))
- grad_nbr2: float32 [1024, 1024], P(None, ('hst', 'dev'))
Inputs may be any that keep to these rules, and one draw needn't show every extreme that they name: Within each cache domain h, plan[h] is a permutation of the 64 block numbers. `miss_ids`: row numbers into the peer's served table; slots at or past the count are unused. `miss_counts`: in every draw some peer is asked for 16 rows by every device. `self_ids`: each names a used fetched slot p * 16 + c of the same device, c below that device's count for peer p. `nbr_ids`: each names a used fetched slot p * 16 + c of the same device, c below that device's count for peer p. `hop_counts`: the first node of every device has 15. `seed_counts`: the first seed of every device has 25.
All inputs are finite; a program needn't handle non-finite values.
Results may differ from a plain program's by a relative error of at most 0.0052.
Values may be sent and summed in bfloat16 or wider, within the bound.
No kernel may reach another device: no remote copies, remote signals or barrier semaphores. Data moves between devices by JAX's collectives and lax.ppermute only.
A program may use at most 128 MiB of HBM per device.

v0:
```python
import jax
import jax.numpy as jnp
from jax import lax
from jax.sharding import PartitionSpec as P

FAN1 = 25
FAN2 = 15
CSLOT = 2
BLOCK = 128


def local_step(
    frontier, self_rows, nbr_rows, count_one, count_two, w_self1, w_nbr1, w_self2, w_nbr2, cot_rows
):
    seed_count = count_two.shape[0]
    width = w_self2.shape[0]
    width_in = frontier.shape[1]
    own_rows = frontier[self_rows]
    mask_one = jnp.arange(FAN2, dtype=jnp.int32)[None, :] < count_one[:, None]
    summed_one = jnp.zeros((own_rows.shape[0], width_in), jnp.float32)
    for k in range(FAN2):
        picked = frontier[nbr_rows[:, k]].astype(jnp.float32)
        summed_one = summed_one + jnp.where(mask_one[:, k][:, None], picked, jnp.zeros_like(picked))
    mean_one = (summed_one / count_one[:, None].astype(jnp.float32)).astype(jnp.bfloat16)
    hidden_pre = jnp.dot(own_rows, w_self1, preferred_element_type=jnp.float32) + jnp.dot(
        mean_one, w_nbr1, preferred_element_type=jnp.float32
    )
    hidden_one = jax.nn.silu(hidden_pre).astype(jnp.bfloat16)
    seed_rows = hidden_one[:seed_count]
    hop_rows = hidden_one[seed_count:].reshape(seed_count, FAN1, width)
    mask_two = jnp.arange(FAN1, dtype=jnp.int32)[None, :] < count_two[:, None]
    summed_two = jnp.einsum(
        "skh,sk->sh", hop_rows, mask_two.astype(jnp.bfloat16), preferred_element_type=jnp.float32
    )
    mean_two = (summed_two / count_two[:, None].astype(jnp.float32)).astype(jnp.bfloat16)
    embedding = (
        jnp.dot(seed_rows, w_self2, preferred_element_type=jnp.float32)
        + jnp.dot(mean_two, w_nbr2, preferred_element_type=jnp.float32)
    ).astype(jnp.bfloat16)
    grad_self2 = jnp.dot(cot_rows.T, seed_rows, preferred_element_type=jnp.float32)
    grad_nbr2 = jnp.dot(cot_rows.T, mean_two, preferred_element_type=jnp.float32)
    back_self = jnp.dot(cot_rows, w_self2.T, preferred_element_type=jnp.float32)
    back_mean = jnp.dot(cot_rows, w_nbr2.T, preferred_element_type=jnp.float32) / count_two[
        :, None
    ].astype(jnp.float32)
    back_hop = back_mean[:, None, :] * mask_two.astype(jnp.float32)[:, :, None]
    back_hidden = jnp.concatenate([back_self, back_hop.reshape(seed_count * FAN1, width)], 0)
    gate_value = jax.nn.sigmoid(hidden_pre)
    back_pre = (back_hidden * gate_value * (1.0 + hidden_pre * (1.0 - gate_value))).astype(
        jnp.bfloat16
    )
    grad_self1 = jnp.dot(back_pre.T, own_rows, preferred_element_type=jnp.float32)
    grad_nbr1 = jnp.dot(back_pre.T, mean_one, preferred_element_type=jnp.float32)
    return (embedding, (grad_self1, grad_nbr1, grad_self2, grad_nbr2))


def local(
    features,
    cache_blocks,
    plan,
    miss_ids,
    miss_counts,
    self_ids,
    nbr_ids,
    hop_counts,
    seed_counts,
    w_self1,
    w_nbr1,
    w_self2,
    w_nbr2,
    cotangent,
):
    width_in = features.shape[1]
    slot_count = miss_ids.shape[3]
    device_count = lax.axis_size(("hst", "dev"))
    start_cache = jnp.zeros((CSLOT, BLOCK, width_in), jnp.bfloat16)
    current = start_cache
    shard_rows = lax.all_gather(cache_blocks, "dev", axis=1, tiled=True)
    block_count = shard_rows.shape[1] // BLOCK
    arrived = shard_rows[0].reshape(block_count, BLOCK, width_in)
    for target in range(CSLOT):
        offset = plan[0, target]
        inside = (offset >= 0) & (offset < block_count)
        chosen = lax.dynamic_index_in_dim(
            arrived, jnp.clip(offset, 0, block_count - 1), 0, keepdims=False
        )
        current = current.at[target].set(jnp.where(inside, chosen, current[target]))
    new_cache = current.reshape(1, CSLOT * BLOCK, width_in)
    lookup_table = jnp.concatenate([features, new_cache[0]], 0)
    requests = miss_ids.reshape(device_count, slot_count)
    row_data = lookup_table[
        lax.all_to_all(requests, ("hst", "dev"), split_axis=0, concat_axis=0, tiled=True)
    ]
    fetched = lax.all_to_all(row_data, ("hst", "dev"), split_axis=0, concat_axis=0, tiled=True)
    counted = miss_counts.reshape(device_count)
    is_valid = jnp.arange(slot_count, dtype=jnp.int32)[None, :] < counted[:, None]
    fetched = jnp.where(is_valid[:, :, None], fetched, jnp.zeros_like(fetched))
    frontier = fetched.reshape(device_count * slot_count, width_in)
    embedding, grads = local_step(
        frontier,
        self_ids,
        nbr_ids,
        hop_counts,
        seed_counts,
        w_self1,
        w_nbr1,
        w_self2,
        w_nbr2,
        cotangent,
    )
    share_self1, share_nbr1, share_self2, share_nbr2 = (
        lax.psum_scatter(grads[0], ("hst", "dev"), scatter_dimension=0, tiled=True),
        lax.psum_scatter(grads[1], ("hst", "dev"), scatter_dimension=0, tiled=True),
        lax.psum_scatter(grads[2], ("hst", "dev"), scatter_dimension=0, tiled=True),
        lax.psum_scatter(grads[3], ("hst", "dev"), scatter_dimension=0, tiled=True),
    )
    return (embedding, new_cache, share_self1.T, share_nbr1.T, share_self2.T, share_nbr2.T)


def solution(mesh):
    return jax.shard_map(
        local,
        mesh=mesh,
        in_specs=(
            P(("hst", "dev"), None),
            P("hst", "dev", None),
            P("hst", "dev"),
            P(("hst", "dev"), None, None, None),
            P(("hst", "dev"), None, None),
            P(("hst", "dev")),
            P(("hst", "dev"), None),
            P(("hst", "dev")),
            P(("hst", "dev")),
            P(),
            P(),
            P(),
            P(),
            P(("hst", "dev"), None),
        ),
        out_specs=(
            P(("hst", "dev"), None),
            P("hst", "dev", None),
            P(None, ("hst", "dev")),
            P(None, ("hst", "dev")),
            P(None, ("hst", "dev")),
            P(None, ("hst", "dev")),
        ),
        check_vma=False,
    )
```

profile of v0, /device:TPU:0, one launch (start us, length us, event | category | flops | bytes accessed | tf_op | source)
XLA Modules:
  0.0 2006.0 jit_solution(17963824004215073880)
XLA Ops:
  7.9 1.5 copy.32
  9.4 11.2 all-to-all-start
  20.6 1.3 fusion.28
  27.9 1.9 all-to-all-done
  29.9 45.5 %all-gather.2.cloned.1.call-done = bf16[1,8192,768]{2,1,0:T(8,128)(2,1)} async-done(((bf16[1,256,768]{2,1,0:T(8,128)(2,1)}), bf16[1,8192,768]{2,1,0:T(8,128)(2,1)}) %all-gather.2.cloned.1.call-update) | async-done | bytes 12582928 | tf_op jit(solution)/shard_map/all_gather | solution.py:78
  77.3 3.9 pad_maximum_fusion
  81.3 12.6 gather_fusion
  93.8 8.7 all-to-all-start.1
  102.6 2.3 convolution_divide_fusion
  104.9 2.6 mul.30
  107.5 4.1 mul.31
  113.0 1.4 fusion.30
  114.4 3.9 broadcast_multiply_fusion
  118.3 25.5 %all-to-all-done.1 = bf16[128,16,768]{2,1,0:T(8,128)(2,1)} async-done(((bf16[128,16,768]{2,1,0:T(8,128)(2,1)}), bf16[128,16,768]{2,1,0:T(8,128)(2,1)}, u32[]{:S(2)}, u32[]{:S(2)}) %all-to-all-start.1) | async-done | bytes 3145760 | tf_op jit(solution)/shard_map/all_to_all | solution.py:94
  143.8 3.3 broadcast_select_fusion
  147.1 6.7 gather_fusion.10
  153.8 7.1 gather_fusion.11
  160.9 7.1 gather_fusion.12
  168.0 7.1 gather_fusion.13
  175.1 7.1 gather_fusion.14
  182.2 7.1 gather_fusion.15
  189.2 7.1 gather_fusion.16
  196.3 7.3 gather_fusion.3
  203.6 7.1 gather_fusion.4
  210.6 7.1 gather_fusion.5
  217.7 7.1 gather_fusion.6
  224.8 7.1 gather_fusion.7
  231.9 7.1 gather_fusion.8
  239.0 7.1 gather_fusion.9
  246.0 7.1 gather_fusion.2
  253.1 7.3 gather_fusion.1
  260.5 3.4 fusion.29
  264.9 8.8 divide_convert_fusion
  273.8 3.9 fusion.1
  278.8 3.5 fusion.32
  283.6 5.1 fusion.31
  288.8 2.7 slice.226
  291.5 2.7 reshape.186
  294.2 2.0 fusion.4
  296.2 2.8 convolution_bitcast_fusion
  299.0 5.4 copy.35
  304.5 3.6 convolution_bitcast_fusion.1
  308.1 5.4 copy.33
  313.5 1.5 fusion.7
  316.3 172.0 %reduce-scatter.11.cloned.1.call-done = f32[8,768]{1,0:T(8,128)} async-done(((f32[1024,768]{1,0:T(8,128)}), f32[8,768]{1,0:T(8,128)}) %reduce-scatter.11.cloned.1.call-update) | async-done | bytes 24592 | tf_op jit(solution)/shard_map/reduce_scatter | solution.py:113
  488.3 213.3 %reduce-scatter.9.cloned.1.call-done = f32[8,768]{1,0:T(8,128)} async-done(((f32[1024,768]{1,0:T(8,128)}), f32[8,768]{1,0:T(8,128)}) %reduce-scatter.9.cloned.1.call-update) | async-done | bytes 24592 | tf_op jit(solution)/shard_map/reduce_scatter | solution.py:112
  701.6 650.9 %reduce-scatter.15.cloned.1.call-done = f32[8,1024]{1,0:T(8,128)} async-done(((f32[1024,1024]{1,0:T(8,128)}), f32[8,1024]{1,0:T(8,128)}) %reduce-scatter.15.cloned.1.call-update) | async-done | bytes 32784
  1352.5 646.7 %reduce-scatter.13.cloned.1.call-done = f32[8,1024]{1,0:T(8,128)} async-done(((f32[1024,1024]{1,0:T(8,128)}), f32[8,1024]{1,0:T(8,128)}) %reduce-scatter.13.cloned.1.call-update) | async-done | bytes 32784
  (87 shorter events, 10.9 us)
Async XLA Ops:
  7.2 105.8 %copy-start = (bf16[1024,1024]{1,0:T(8,128)(2,1)S(1)}, bf16[1024,1024]{1,0:T(8,128)(2,1)}, u32[]{:S(2)}) copy-start(bf16[1024,1024]{1,0:T(8,128)(2,1)} %param.29) | copy-start | bytes 6291460
  7.2 68.3 %all-gather.2.cloned.1.call-start = ((), (), s32[]{:S(2)}) async-start(), calls=%async_computation.6 | async-start | bytes 12976128 | tf_op jit(solution)/shard_map/all_gather | solution.py:78
  9.4 20.4 %all-to-all-start = ((s32[128,1,16]{2,1,0:T(1,128)}), s32[128,1,16]{2,1,0:T(1,128)S(1)}, u32[]{:S(2)}, u32[]{:S(2)}) async-start(s32[128,1,16]{2,1,0:T(1,128)} %bitcast.6), calls=%async_computation | async-start | bytes 131072 | tf_op jit(solution)/shard_map/all_to_all | solution.py:92
  76.6 0.7 copy-start.10
  93.8 8.8 copy-start.12
  93.8 50.0 %all-to-all-start.1 = ((bf16[128,16,768]{2,1,0:T(8,128)(2,1)}), bf16[128,16,768]{2,1,0:T(8,128)(2,1)}, u32[]{:S(2)}, u32[]{:S(2)}) async-start(bf16[128,16,768]{2,1,0:T(8,128)(2,1)} %bitcast.66), calls=%async_computation.1 | async-start | bytes 6291456 | tf_op jit(solution)/shard_map/all_to_all | solution.py:94
  102.6 385.7 %reduce-scatter.11.cloned.1.call-start = ((), (), s32[]{:S(2)}) async-start(), calls=%async_computation.8 | async-start | bytes 3170304 | tf_op jit(solution)/shard_map/reduce_scatter | solution.py:113
  107.5 4.1 copy-start.23
  107.5 4.3 copy-start.14
  107.5 4.5 copy-start.22
  107.5 4.6 copy-start.15
  260.4 3.5 copy-start.2
  260.4 3.6 copy-start.3
  260.4 3.6 copy-start.4
  260.4 3.6 copy-start.5
  260.4 3.7 copy-start.6
  260.4 4.1 copy-start.7
  260.5 4.4 copy-start.8
  260.5 4.4 copy-start.16
  260.5 4.4 copy-start.17
  260.5 4.4 copy-start.18
  260.5 4.4 copy-start.19
  260.5 4.4 copy-start.20
  260.5 4.4 copy-start.21
  264.9 8.8 copy-start.9
  264.9 8.8 copy-start.13
  264.9 8.8 copy-start.24
  277.6 1.2 copy-start.25
  282.3 1.3 copy-start.11
  282.4 419.2 %reduce-scatter.9.cloned.1.call-start = ((), (), s32[]{:S(2)}) async-start(), calls=%async_computation.7 | async-start | bytes 3170304 | tf_op jit(solution)/shard_map/reduce_scatter | solution.py:112
  288.7 1063.8 %reduce-scatter.15.cloned.1.call-start = ((), (), s32[]{:S(2)}) async-start(), calls=%async_computation.10 | async-start | bytes 4227072
  304.4 1694.8 %reduce-scatter.13.cloned.1.call-start = ((), (), s32[]{:S(2)}) async-start(), calls=%async_computation.9 | async-start | bytes 4227072
  313.5 1.6 copy-start.1
Sparse Core Ops, SparseCore 0:
  10.2 65.1 all-gather.1
  282.5 205.7 reduce-scatter.10
  493.7 207.9 reduce-scatter.8
  704.4 648.0 reduce-scatter.14
  1355.3 643.8 reduce-scatter.12
where the time goes:
time: 2010 us
  waiting for transfers between devices  1760 us (88%)
  local copies, waits for them, and re-layouts  158 us (8%)
  matrix products  30.5 us (2%)
  other arithmetic  22.8 us (1%)
  starting transfers between devices  20.1 us (1%)
    unnamed x7, waiting for transfers between devices  1300 us
    reduce_scatter x1, waiting for transfers between devices, local(): lax.psum_scatter(grads[0], ('hst', 'dev'), scatter_dimension=0, tiled=True)  213 us
    reduce_scatter x1, waiting for transfers between devices, local(): lax.psum_scatter(grads[1], ('hst', 'dev'), scatter_dimension=0, tiled=True)  172 us
    gather x15, local copies, waits for them, and re-layouts, local_step(): picked = frontier[nbr_rows[:, k]].astype(jnp.float32)  106 us
    all_gather x1, waiting for transfers between devices, local(): shard_rows = lax.all_gather(cache_blocks, 'dev', axis=1, tiled=True)  45.5 us
  transfers between devices with their start and end apart: 7, of which 7 were waited for; matrix products, arithmetic and copies ran while one was open for 3% of the time, Pallas kernels for 0%

commit v1 on v0

--- a/solution.py
+++ b/solution.py
@@ -75,7 +75,12 @@
     device_count = lax.axis_size(("hst", "dev"))
     start_cache = jnp.zeros((CSLOT, BLOCK, width_in), jnp.bfloat16)
     current = start_cache
-    shard_rows = lax.all_gather(cache_blocks, "dev", axis=1, tiled=True)
+    shard_rows = jnp.concatenate(
+        jax.lax.all_to_all(
+            jnp.stack([cache_blocks for _ in range(jax.lax.axis_size("dev"))]), "dev", 0, 0
+        ),
+        axis=1,
+    )
     block_count = shard_rows.shape[1] // BLOCK
     arrived = shard_rows[0].reshape(block_count, BLOCK, width_in)
     for target in range(CSLOT):

time: 2010 us -> 2140 us (1.065)
  waiting for transfers between devices: 1760 us -> 1860 us
    all_to_all x1, waiting for transfers between devices: 1.92 us -> 156 us  [local(): jax.lax.all_to_all(jnp.stack([cache_blocks for _ in range(jax.lax.axis_si...]
    all_gather x1 -> x0, waiting for transfers between devices: 45.5 us -> none  [local(): shard_rows = lax.all_gather(cache_blocks, 'dev', axis=1, tiled=True)]
    unnamed x7 -> x6, waiting for transfers between devices: 1300 us -> 1300 us
  transfers between devices with their start and end apart: 7 -> 6, of which waited for: 7 -> 6; matrix products, arithmetic and copies ran while one was open for 3% -> 2% of each run, Pallas kernels for 0% -> 0%
where the time goes in v1:
time: 2140 us; the launch traced here: 2130 us
  waiting for transfers between devices  1860 us (87%)
  local copies, waits for them, and re-layouts  163 us (8%)
  matrix products  30.5 us (1%)
    unnamed x6, waiting for transfers between devices  1300 us
    reduce_scatter x1, waiting for transfers between devices, local(): lax.psum_scatter(grads[0], ('hst', 'dev'), scatter_dimension=0, tiled=True)  213 us
    reduce_scatter x1, waiting for transfers between devices, local(): lax.psum_scatter(grads[1], ('hst', 'dev'), scatter_dimension=0, tiled=True)  172 us
    all_to_all x1, waiting for transfers between devices, local(): jax.lax.all_to_all(jnp.stack([cache_blocks for _ in range(jax.lax.axis_si...  156 us
    gather x15, local copies, waits for them, and re-layouts, local_step(): picked = frontier[nbr_rows[:, k]].astype(jnp.float32)  106 us
  transfers between devices with their start and end apart: 6, of which 6 were waited for; matrix products, arithmetic and copies ran while one was open for 2% of the time, Pallas kernels for 0%

profile of v1, /device:TPU:0, one launch (start us, length us, event | category | flops | bytes accessed | tf_op | source)
XLA Modules:
  0.0 2129.3 jit_solution(14187907152749012379)
XLA Ops:
  8.2 20.3 all_to_all.22
  28.5 6.9 stack.2
  35.4 5.2 all-to-all-start
  45.3 155.7 %all-to-all-done = bf16[32,1,256,768]{3,2,1,0:T(8,128)(2,1)} async-done(((bf16[32,1,256,768]{3,2,1,0:T(8,128)(2,1)}), bf16[32,1,256,768]{3,2,1,0:T(8,128)(2,1)}, u32[]{:S(2)}, u32[]{:S(2)}) %all-to-all-start) | async-done | bytes 12582944 | tf_op jit(solution)/shard_map/all_to_all | solution.py:79
  202.8 3.9 pad_maximum_fusion
  206.8 12.6 gather_fusion
  219.3 5.9 all-to-all-start.2
  225.3 2.3 convolution_divide_fusion
  227.6 2.6 mul.30
  230.2 4.1 mul.31
  235.6 1.4 fusion.30
  237.0 3.9 broadcast_multiply_fusion
  240.9 25.6 %all-to-all-done.2 = bf16[128,16,768]{2,1,0:T(8,128)(2,1)} async-done(((bf16[128,16,768]{2,1,0:T(8,128)(2,1)}), bf16[128,16,768]{2,1,0:T(8,128)(2,1)}, u32[]{:S(2)}, u32[]{:S(2)}) %all-to-all-start.2) | async-done | bytes 3145760 | tf_op jit(solution)/shard_map/all_to_all | solution.py:99
  266.4 3.3 broadcast_select_fusion
  269.7 6.7 gather_fusion.10
  276.5 7.1 gather_fusion.11
  283.6 7.1 gather_fusion.12
  290.6 7.1 gather_fusion.13
  297.7 7.1 gather_fusion.14
  304.8 7.1 gather_fusion.15
  311.9 7.1 gather_fusion.16
  319.0 7.3 gather_fusion.3
  326.2 7.1 gather_fusion.4
  333.3 7.1 gather_fusion.5
  340.4 7.1 gather_fusion.6
  347.4 7.1 gather_fusion.7
  354.5 7.1 gather_fusion.8
  361.6 7.1 gather_fusion.9
  368.7 7.1 gather_fusion.2
  375.8 7.3 gather_fusion.1
  383.2 3.4 fusion.29
  387.6 8.8 divide_convert_fusion
  396.4 3.9 fusion.1
  401.4 3.5 fusion.32
  405.1 1.2 copy-done.11
  406.3 5.1 fusion.31
  411.4 2.7 slice.226
  414.1 2.7 reshape.189
  416.9 2.0 fusion.4
  418.9 2.8 convolution_bitcast_fusion
  421.7 5.4 copy.35
  427.2 3.6 convolution_bitcast_fusion.1
  430.7 5.4 copy.33
  436.1 1.5 fusion.7
  438.9 172.1 %reduce-scatter.11.cloned.1.call-done = f32[8,768]{1,0:T(8,128)} async-done(((f32[1024,768]{1,0:T(8,128)}), f32[8,768]{1,0:T(8,128)}) %reduce-scatter.11.cloned.1.call-update) | async-done | bytes 24592 | tf_op jit(solution)/shard_map/reduce_scatter | solution.py:118
  611.0 213.4 %reduce-scatter.9.cloned.1.call-done = f32[8,768]{1,0:T(8,128)} async-done(((f32[1024,768]{1,0:T(8,128)}), f32[8,768]{1,0:T(8,128)}) %reduce-scatter.9.cloned.1.call-update) | async-done | bytes 24592 | tf_op jit(solution)/shard_map/reduce_scatter | solution.py:117
  824.4 651.3 %reduce-scatter.15.cloned.1.call-done = f32[8,1024]{1,0:T(8,128)} async-done(((f32[1024,1024]{1,0:T(8,128)}), f32[8,1024]{1,0:T(8,128)}) %reduce-scatter.15.cloned.1.call-update) | async-done | bytes 32784
  1475.6 646.9 %reduce-scatter.13.cloned.1.call-done = f32[8,1024]{1,0:T(8,128)} async-done(((f32[1024,1024]{1,0:T(8,128)}), f32[8,1024]{1,0:T(8,128)}) %reduce-scatter.13.cloned.1.call-update) | async-done | bytes 32784
  (90 shorter events, 8.5 us)
Async XLA Ops:
  7.2 228.4 %copy-start = (bf16[1024,1024]{1,0:T(8,128)(2,1)S(1)}, bf16[1024,1024]{1,0:T(8,128)(2,1)}, u32[]{:S(2)}) copy-start(bf16[1024,1024]{1,0:T(8,128)(2,1)} %param.29) | copy-start | bytes 6291460
  35.4 5.2 copy-start.24
  35.4 9.7 copy-start.23
  35.4 9.8 copy-start.15
  35.4 9.8 copy-start.25
  35.4 165.6 %all-to-all-start = ((bf16[32,1,256,768]{3,2,1,0:T(8,128)(2,1)}), bf16[32,1,256,768]{3,2,1,0:T(8,128)(2,1)}, u32[]{:S(2)}, u32[]{:S(2)}) async-start(bf16[32,1,256,768]{3,2,1,0:T(8,128)(2,1)} %stack.2), calls=%async_computation | async-start | bytes 25165824 | tf_op jit(solution)/shard_map/all_to_all | solution.py:79
  202.1 0.7 copy-start.10
  219.3 5.9 copy-start.12
  219.3 47.1 %all-to-all-start.2 = ((bf16[128,16,768]{2,1,0:T(8,128)(2,1)}), bf16[128,16,768]{2,1,0:T(8,128)(2,1)}, u32[]{:S(2)}, u32[]{:S(2)}) async-start(bf16[128,16,768]{2,1,0:T(8,128)(2,1)} %bitcast.67), calls=%async_computation.2 | async-start | bytes 6291456 | tf_op jit(solution)/shard_map/all_to_all | solution.py:99
  225.2 385.8 %reduce-scatter.11.cloned.1.call-start = ((), (), s32[]{:S(2)}) async-start(), calls=%async_computation.8 | async-start | bytes 3170304 | tf_op jit(solution)/shard_map/reduce_scatter | solution.py:118
  230.2 4.2 copy-start.14
  230.2 4.5 copy-start.22
  383.1 3.5 copy-start.2
  383.1 3.6 copy-start.3
  383.1 3.6 copy-start.4
  383.1 3.6 copy-start.5
  383.1 3.7 copy-start.6
  383.1 4.1 copy-start.7
  383.1 4.4 copy-start.8
  383.1 4.4 copy-start.16
  383.1 4.4 copy-start.17
  383.1 4.4 copy-start.18
  383.1 4.4 copy-start.19
  383.2 4.4 copy-start.20
  383.2 4.4 copy-start.21
  387.5 8.8 copy-start.9
  387.5 8.8 copy-start.13
  387.6 8.8 copy-start.26
  400.3 1.2 copy-start.27
  405.0 1.3 copy-start.11
  405.0 419.4 %reduce-scatter.9.cloned.1.call-start = ((), (), s32[]{:S(2)}) async-start(), calls=%async_computation.7 | async-start | bytes 3170304 | tf_op jit(solution)/shard_map/reduce_scatter | solution.py:117
  411.4 1064.3 %reduce-scatter.15.cloned.1.call-start = ((), (), s32[]{:S(2)}) async-start(), calls=%async_computation.10 | async-start | bytes 4227072
  427.1 1695.4 %reduce-scatter.13.cloned.1.call-start = ((), (), s32[]{:S(2)}) async-start(), calls=%async_computation.9 | async-start | bytes 4227072
  436.1 1.6 copy-start.1
Sparse Core Ops, SparseCore 0:
  405.1 205.8 reduce-scatter.10
  616.3 207.9 reduce-scatter.8
  827.3 648.3 reduce-scatter.14
  1478.4 644.0 reduce-scatter.12
